TPU v7x, 32 devices: a whole 2x2x4 slice. The times are simulated.
32 devices in a mesh: dp: 16 (over z, y, x), cls: 2 (over core).
Axes of the slice: x: 2, y: 2, z: 4, core: 2. Of those that a mesh axis runs over, the one named last changes fastest.
Arguments:
- features: bfloat16 [3072, 2048], P('dp'), may hold values from -128 to 128
- labels: int32 [3072], P('dp'), may hold values from 0 to 16383
- weight: bfloat16 [2048, 16384], P('dp', 'cls'), may hold values from -1 to 1
- noise: float32 [16, 2, 1024, 1024], P('dp', 'cls'), may hold values from -6 to 6
Outputs:
- noisy_grad: float32 [16, 2, 1024, 1024], P('dp', 'cls')
All inputs are finite; a program needn't handle non-finite values.
Results may differ from a plain program's by a relative error of at most 0.0017.
Values may be sent and summed in bfloat16 or wider, within the bound.
A program may use at most 128 MiB of HBM per device.

v0:
```python
import jax
import jax.numpy as jnp
from jax import lax
from jax.sharding import PartitionSpec as P

CSPLIT = 8
CLIP_NORM = 40.0
NOISE_STD = 0.4


def on_device(features, labels, weight, noise):
    tok_rows = features.shape[0]
    feature_dim = features.shape[1]
    class_shard = weight.shape[1]
    groups = lax.axis_size("dp") // CSPLIT
    row_block = feature_dim // groups
    col_block = class_shard // CSPLIT
    slot_count = groups * CSPLIT
    feature_slots = jnp.broadcast_to(
        features.reshape(tok_rows, groups, 1, row_block), (tok_rows, groups, CSPLIT, row_block)
    ).reshape(tok_rows, slot_count, row_block)
    logits = jnp.dot(
        features,
        lax.all_gather(weight, "dp", axis=0, tiled=True),
        preferred_element_type=jnp.float32,
    )
    offset = labels - lax.axis_index("cls") * class_shard
    label_hit = lax.broadcasted_iota(jnp.int32, (tok_rows, class_shard), 1) == offset[:, None]
    onehot = label_hit.astype(jnp.float32)
    local_max = jnp.max(logits, axis=1)
    exponent = jnp.exp(logits - local_max[:, None])
    row_total = jnp.sum(exponent, axis=1)
    row_square = jnp.sum(exponent * exponent, axis=1)
    picked = jnp.sum(onehot * logits, axis=1)
    global_max = lax.pmax(local_max, "cls")
    rescale = jnp.exp(local_max - global_max)
    row_total, row_square, picked = lax.psum(
        (row_total * rescale, row_square * rescale * rescale, picked), "cls"
    )
    softmax = exponent * (jnp.exp(local_max - global_max) / row_total)[:, None]
    label_prob = jnp.exp(picked - global_max) / row_total
    spread = row_square / (row_total * row_total) - 2.0 * label_prob + 1.0
    energy = jnp.sum(jnp.square(features.astype(jnp.float32)), axis=1)
    factor = CLIP_NORM * lax.rsqrt(jnp.maximum(energy * spread, CLIP_NORM * CLIP_NORM))
    weighted = (factor[:, None] * (softmax - onehot)).astype(jnp.bfloat16)
    coef_slots = jnp.broadcast_to(
        weighted.reshape(tok_rows, 1, CSPLIT, col_block), (tok_rows, groups, CSPLIT, col_block)
    ).reshape(tok_rows, slot_count, col_block)
    feature_recv, coef_recv = (
        lax.all_to_all(feature_slots, "dp", split_axis=1, concat_axis=1, tiled=True),
        lax.all_to_all(coef_slots, "dp", split_axis=1, concat_axis=1, tiled=True),
    )
    grad_block = lax.dot_general(
        feature_recv, coef_recv, (((0, 1), (0, 1)), ((), ())), preferred_element_type=jnp.float32
    )
    return (grad_block + NOISE_STD * noise[0, 0]).reshape(noise.shape)


def solution(mesh):
    placed = (P("dp", None), P("dp"), P("dp", "cls"), P("dp", "cls", None, None))
    return jax.shard_map(
        on_device, mesh=mesh, in_specs=placed, out_specs=P("dp", "cls", None, None), check_vma=False
    )
```

profile of v0, /device:TPU:28, one launch (start us, length us, event | category | flops | bytes accessed | tf_op | source)
XLA Modules:
  0.0 691.1 jit_solution(1169559670547436324)
XLA Ops:
  6.5 0.0 all-gather.2.cloned.1.call-start
  6.5 0.7 all-gather.2.cloned.1.call-update
  7.3 1.2 copy.14
  8.5 3.4 broadcast_in_dim.21
  11.8 0.0 copy-start
  11.9 0.0 copy-start.1
  11.9 7.1 %all-to-all-start.1 = ((bf16[192,16,1024]{2,0,1:T(8,128)(2,1)}), bf16[192,16,1024]{2,0,1:T(8,128)(2,1)}, u32[]{:S(2)}, u32[]{:S(2)}) async-start(bf16[192,16,1024]{2,0,1:T(8,128)(2,1)} %bitcast.24), calls=%async_computation.1 | async-start | bytes 12582912 | tf_op jit(solution)/shard_map/all_to_all | solution.py:50
  18.9 0.0 copy-done
  18.9 0.2 multiply_reduce_fusion.1
  19.2 0.0 copy-done.1
  19.2 463.0 %all-gather.2.cloned.1.call-done = bf16[2048,8192]{1,0:T(8,128)(2,1)} async-done(((bf16[128,8192]{1,0:T(8,128)(2,1)}), bf16[2048,8192]{1,0:T(8,128)(2,1)}) %all-gather.2.cloned.1.call-update) | async-done | bytes 33554448 | tf_op jit(solution)/shard_map/all_gather | solution.py:24
  482.2 16.4 %fusion.4 = (f32[192]{0:T(256)S(1)}, f32[192,8192]{1,0:T(8,128)}) fusion(bf16[192,2048]{1,0:T(8,128)(2,1)S(1)} %copy-done, bf16[2048,8192]{1,0:T(8,128)(2,1)} %all-gather.2.cloned.1.call-done), kind=kOutput, calls=%fused_computation.18 | convolution fusion | flops 6444023808 | bytes 40633088 | tf_op jit(solution)/shard_map/dot_general | solution.py:22
  498.6 2.4 pmax.7
  501.1 4.2 multiply_reduce_fusion
  505.3 2.5 all-reduce
  507.8 4.0 multiply_convert_fusion
  511.8 0.4 copy.13
  512.2 0.0 all-to-all-done.1
  512.2 3.6 broadcast_in_dim.9
  515.9 6.8 all-to-all-start
  522.7 5.3 copy.7
  528.1 138.2 %all-to-all-done = bf16[192,16,1024]{2,0,1:T(8,128)(2,1)} async-done(((bf16[192,16,1024]{2,0,1:T(8,128)(2,1)}), bf16[192,16,1024]{2,0,1:T(8,128)(2,1)}, u32[]{:S(2)}, u32[]{:S(2)}) %all-to-all-start) | async-done | bytes 6291488 | tf_op jit(solution)/shard_map/all_to_all | solution.py:51
  666.3 12.7 %fusion.1 = f32[1,1,1024,1024]{2,3,1,0:T(8,128)} fusion(f32[1,1,1024,1024]{2,3,1,0:T(8,128)} %copy.7, bf16[192,16,1024]{2,0,1:T(8,128)(2,1)} %all-to-all-done, bf16[192,16,1024]{2,0,1:T(8,128)(2,1)} %all-to-all-done.1), kind=kOutput, calls=%fused_computation.7 | convolution fusion | flops 6444548096 | bytes 20971520 | tf_op jit(solution)/shard_map/dot_general | solution.py:53
  679.0 5.3 copy.8
  (3 shorter events, 0.0 us)
Async XLA Ops:
  6.5 475.7 %all-gather.2.cloned.1.call-start = ((), (), s32[]{:S(2)}) async-start(), calls=%async_computation.2 | async-start | bytes 35651584 | tf_op jit(solution)/shard_map/all_gather | solution.py:24
  11.8 7.1 %copy-start = (bf16[192,2048]{1,0:T(8,128)(2,1)S(1)}, bf16[192,2048]{1,0:T(8,128)(2,1)}, u32[]{:S(2)}) copy-start(bf16[192,2048]{1,0:T(8,128)(2,1)} %param.4) | copy-start | bytes 2359300
  11.9 7.3 %copy-start.1 = (s32[192]{0:T(256)S(1)}, s32[192]{0:T(256)}, u32[]{:S(2)}) copy-start(s32[192]{0:T(256)} %param.5) | copy-start | bytes 2308
  11.9 500.4 %all-to-all-start.1 = ((bf16[192,16,1024]{2,0,1:T(8,128)(2,1)}), bf16[192,16,1024]{2,0,1:T(8,128)(2,1)}, u32[]{:S(2)}, u32[]{:S(2)}) async-start(bf16[192,16,1024]{2,0,1:T(8,128)(2,1)} %bitcast.24), calls=%async_computation.1 | async-start | bytes 12582912 | tf_op jit(solution)/shard_map/all_to_all | solution.py:50
  515.9 150.4 %all-to-all-start = ((bf16[192,16,1024]{2,0,1:T(8,128)(2,1)}), bf16[192,16,1024]{2,0,1:T(8,128)(2,1)}, u32[]{:S(2)}, u32[]{:S(2)}) async-start(bf16[192,16,1024]{2,0,1:T(8,128)(2,1)} %bitcast.25), calls=%async_computation | async-start | bytes 12582912 | tf_op jit(solution)/shard_map/all_to_all | solution.py:51
Sparse Core Ops, SparseCore 0:
  10.1 472.0 all-gather.1
where the time goes:
time: 692 us; the launch traced here: 691 us
  waiting for transfers between devices  602 us (87%)
  matrix products  29.1 us (4%)
  local copies, waits for them, and re-layouts  19.3 us (3%)
  starting transfers between devices  13.9 us (2%)
  between operations  13.4 us (2%)
  other arithmetic  8.47 us (1%)
    all_gather x1, waiting for transfers between devices, on_device(): lax.all_gather(weight, 'dp', axis=0, tiled=True)  463 us
    all_to_all x1, waiting for transfers between devices, on_device(): lax.all_to_all(coef_slots, 'dp', split_axis=1, concat_axis=1, tiled=True)  138 us
    dot_general x1, matrix products, on_device(): jnp.dot(features, lax.all_gather(weight, 'dp', axis=0, tiled=True), prefe...  16.4 us
  transfers between devices with their start and end apart: 3, of which 2 were waited for; matrix products, arithmetic and copies ran while one was open for 5% of the time, Pallas kernels for 0%

commit v1 on v0

--- a/solution.py
+++ b/solution.py
@@ -6,6 +6,27 @@
 CSPLIT = 8
 CLIP_NORM = 40.0
 NOISE_STD = 0.4
+
+
+def laid_out(blocks, dim):
+    shape = list(blocks.shape[1:])
+    shape[dim] *= blocks.shape[0]
+    return jnp.moveaxis(blocks, 0, dim).reshape(shape)
+
+
+def grow_blocks(x, axis):
+    size, here = (lax.axis_size(axis), lax.axis_index(axis))
+    blocks, distance = (x[None], 1)
+    while distance < size:
+        other = lax.ppermute(blocks, axis, [(i, i ^ distance) for i in range(size)])
+        low = here & distance == 0
+        blocks = jnp.concatenate([jnp.where(low, blocks, other), jnp.where(low, other, blocks)])
+        distance *= 2
+    return blocks
+
+
+def doubled_up(x, axis, dim):
+    return laid_out(grow_blocks(x, axis), dim)
 
 
 def on_device(features, labels, weight, noise):
@@ -19,11 +40,7 @@
     feature_slots = jnp.broadcast_to(
         features.reshape(tok_rows, groups, 1, row_block), (tok_rows, groups, CSPLIT, row_block)
     ).reshape(tok_rows, slot_count, row_block)
-    logits = jnp.dot(
-        features,
-        lax.all_gather(weight, "dp", axis=0, tiled=True),
-        preferred_element_type=jnp.float32,
-    )
+    logits = jnp.dot(features, doubled_up(weight, "dp", 0), preferred_element_type=jnp.float32)
     offset = labels - lax.axis_index("cls") * class_shard
     label_hit = lax.broadcasted_iota(jnp.int32, (tok_rows, class_shard), 1) == offset[:, None]
     onehot = label_hit.astype(jnp.float32)

time: 692 us -> 1390 us (2.01)
  waiting for transfers between devices: 602 us -> 1230 us
  other arithmetic: 8.47 us -> 84.3 us
    ppermute x0 -> x4, waiting for transfers between devices: none -> 1090 us  [grow_blocks(): other = lax.ppermute(blocks, axis, [(i, i ^ distance) for i in range(size)])]
    all_gather x1 -> x0, waiting for transfers between devices: 463 us -> none  [on_device(): lax.all_gather(weight, 'dp', axis=0, tiled=True)]
    concatenate x0 -> x4, other arithmetic: none -> 39.2 us  [grow_blocks(): jnp.concatenate([jnp.where(low, blocks, other), jnp.where(low, other, blo...]
    select_n x0 -> x4, other arithmetic: none -> 36.6 us  [grow_blocks(): jnp.where(low, blocks, other)]
  transfers between devices with their start and end apart: 3 -> 6, of which waited for: 2 -> 5; matrix products, arithmetic and copies ran while one was open for 5% -> 6% of each run, Pallas kernels for 0% -> 0%
where the time goes in v1:
time: 1390 us
  waiting for transfers between devices  1230 us (88%)
  other arithmetic  84.3 us (6%)
  matrix products  28.9 us (2%)
  local copies, waits for them, and re-layouts  23.9 us (2%)
  starting transfers between devices  17 us (1%)
    ppermute x4, waiting for transfers between devices, grow_blocks(): other = lax.ppermute(blocks, axis, [(i, i ^ distance) for i in range(size)])  1090 us
    all_to_all x1, waiting for transfers between devices, on_device(): lax.all_to_all(coef_slots, 'dp', split_axis=1, concat_axis=1, tiled=True)  138 us
    concatenate x4, other arithmetic, grow_blocks(): jnp.concatenate([jnp.where(low, blocks, other), jnp.where(low, other, blo...  39.2 us
    select_n x4, other arithmetic, grow_blocks(): jnp.where(low, blocks, other)  36.6 us
  transfers between devices with their start and end apart: 6, of which 5 were waited for; matrix products, arithmetic and copies ran while one was open for 6% of the time, Pallas kernels for 0%

profile of v1, /device:TPU:28, one launch (start us, length us, event | category | flops | bytes accessed | tf_op | source)
XLA Modules:
  0.0 1390.6 jit_solution(12395224276521630293)
XLA Ops:
  0.0 1.5 collective-permute-start
  1.5 46.2 %collective-permute-done = bf16[1,128,8192]{2,1,0:T(8,128)(2,1)} collective-permute-done((bf16[1,128,8192]{2,1,0:T(8,128)(2,1)}, bf16[1,128,8192]{2,1,0:T(8,128)(2,1)}, u32[]{:S(2)}, u32[]{:S(2)}) %collective-permute-start) | collective-permute-done | bytes 2097184 | tf_op jit(solution)/shard_map/ppermute | solution.py:21
  47.7 2.5 broadcast_select_fusion.7
  50.2 0.0 copy-start.2
  50.2 1.4 copy-done.2
  51.6 2.4 pad_maximum_fusion.3
  53.9 0.5 collective-permute-start.1
  54.4 91.2 %collective-permute-done.1 = bf16[2,128,8192]{2,1,0:T(8,128)(2,1)} collective-permute-done((bf16[2,128,8192]{2,1,0:T(8,128)(2,1)}, bf16[2,128,8192]{2,1,0:T(8,128)(2,1)}, u32[]{:S(2)}, u32[]{:S(2)}) %collective-permute-start.1) | collective-permute-done | bytes 4194336 | tf_op jit(solution)/shard_map/ppermute | solution.py:21
  145.7 5.4 broadcast_select_fusion.5
  151.1 7.4 pad_maximum_fusion.2
  158.5 0.4 collective-permute-start.2
  159.0 180.3 %collective-permute-done.2 = bf16[4,128,8192]{2,1,0:T(8,128)(2,1)} collective-permute-done((bf16[4,128,8192]{2,1,0:T(8,128)(2,1)}, bf16[4,128,8192]{2,1,0:T(8,128)(2,1)}, u32[]{:S(2)}, u32[]{:S(2)}) %collective-permute-start.2) | collective-permute-done | bytes 8388640 | tf_op jit(solution)/shard_map/ppermute | solution.py:21
  339.2 6.3 broadcast_select_fusion.3
  345.6 0.0 copy-start
  345.6 0.0 copy-start.1
  345.6 0.0 copy-start.3
  345.6 6.7 pad_maximum_fusion.1
  352.3 1.6 copy-done
  353.9 2.7 copy-done.1
  356.6 0.3 collective-permute-start.3
  356.9 0.0 copy-done.3
  356.9 0.1 copy.14
  357.0 3.5 broadcast_in_dim.25
  360.5 0.0 copy-start.4
  360.5 7.3 all-to-all-start.1
  367.8 0.2 multiply_reduce_fusion.1
  368.0 0.0 copy-done.4
  368.0 776.0 %collective-permute-done.3 = bf16[8,128,8192]{2,1,0:T(8,128)(2,1)} collective-permute-done((bf16[8,128,8192]{2,1,0:T(8,128)(2,1)}, bf16[8,128,8192]{2,1,0:T(8,128)(2,1)}, u32[]{:S(2)}, u32[]{:S(2)}) %collective-permute-start.3) | collective-permute-done | bytes 16777248 | tf_op jit(solution)/shard_map/ppermute | solution.py:21
  1144.0 22.3 %broadcast_select_fusion.1 = (bf16[8,128,8192]{2,1,0:T(8,128)(2,1)}, bf16[8,128,8192]{2,1,0:T(8,128)(2,1)}) fusion(bf16[8,128,8192]{2,1,0:T(8,128)(2,1)} %collective-permute-done.3, pred[]{:T(512)S(6)} %eq.20, bf16[4,128,8192]{2,1,0:T(8,128)(2,1)} %copy-done.1, bf16[4,128,8192]{2,1,0:T(8,128)(2,1)} %copy-done), kind=kLoop, calls=%fused_computation.3 | loop fusion | flops 25165824 | bytes 67108864 | tf_op jit(solution)/shard_map/jit(_where)/select_n | solution.py:23
  1166.3 22.8 %pad_maximum_fusion = bf16[16,128,8192]{2,1,0:T(8,128)(2,1)} fusion(bf16[8,128,8192]{2,1,0:T(8,128)(2,1)} %get-tuple-element.12, bf16[8,128,8192]{2,1,0:T(8,128)(2,1)} %get-tuple-element.11), kind=kLoop, calls=%fused_computation | loop fusion | flops 16777216 | bytes 67108864 | tf_op jit(solution)/shard_map/concatenate | solution.py:23
  1189.0 16.3 %fusion.6 = (f32[192]{0:T(256)S(1)}, f32[8192,192]{0,1:T(8,128)}) fusion(bf16[192,2048]{1,0:T(8,128)(2,1)S(1)} %copy-done.3, bf16[2048,8192]{1,0:T(8,128)(2,1)} %bitcast.41), kind=kOutput, calls=%fused_computation.32 | convolution fusion | flops 6444023808 | bytes 40633088 | tf_op jit(solution)/shard_map/dot_general | solution.py:43
  1205.4 2.4 pmax.7
  1207.8 4.2 multiply_reduce_fusion
  1212.0 2.5 all-reduce
  1214.5 4.0 multiply_convert_fusion
  1218.5 0.4 copy.13
  1218.9 0.0 all-to-all-done.1
  1219.0 3.6 broadcast_in_dim.23
  1222.5 6.9 all-to-all-start
  1229.5 5.3 copy.7
  1234.8 137.8 %all-to-all-done = bf16[192,16,1024]{2,0,1:T(8,128)(2,1)} async-done(((bf16[192,16,1024]{2,0,1:T(8,128)(2,1)}), bf16[192,16,1024]{2,0,1:T(8,128)(2,1)}, u32[]{:S(2)}, u32[]{:S(2)}) %all-to-all-start) | async-done | bytes 6291488 | tf_op jit(solution)/shard_map/all_to_all | solution.py:68
  1372.6 12.6 fusion.3
  1385.2 5.3 copy.8
  (3 shorter events, 0.0 us)
Async XLA Ops:
  0.0 47.7 %collective-permute-start = (bf16[1,128,8192]{2,1,0:T(8,128)(2,1)}, bf16[1,128,8192]{2,1,0:T(8,128)(2,1)}, u32[]{:S(2)}, u32[]{:S(2)}) collective-permute-start(bf16[1,128,8192]{2,1,0:T(8,128)(2,1)} %bitcast.48), channel_id=1, source_target_pairs={{0,2},{2,0},{4,6},{6,4},{8,10},{10,8},{12,14},{14,12},{16,18},{18,... | collective-permute-start | bytes 6291464 | tf_op jit(solution)/shard_map/ppermute | solution.py:21
  50.2 1.4 copy-start.2
  53.9 91.8 %collective-permute-start.1 = (bf16[2,128,8192]{2,1,0:T(8,128)(2,1)}, bf16[2,128,8192]{2,1,0:T(8,128)(2,1)}, u32[]{:S(2)}, u32[]{:S(2)}) collective-permute-start(bf16[2,128,8192]{2,1,0:T(8,128)(2,1)} %pad_maximum_fusion.3), channel_id=1, source_target_pairs={{0,4},{2,6},{4,0},{6,2},{8,12},{10,14},{12,8},{14,10},{16,20},{18,... | collective-permute-start | bytes 12582920 | tf_op jit(solution)/shard_map/ppermute | solution.py:21
  158.5 180.7 %collective-permute-start.2 = (bf16[4,128,8192]{2,1,0:T(8,128)(2,1)}, bf16[4,128,8192]{2,1,0:T(8,128)(2,1)}, u32[]{:S(2)}, u32[]{:S(2)}) collective-permute-start(bf16[4,128,8192]{2,1,0:T(8,128)(2,1)} %pad_maximum_fusion.2), channel_id=1, source_target_pairs={{0,8},{2,10},{4,12},{6,14},{8,0},{10,2},{12,4},{14,6},{16,24},{18,... | collective-permute-start | bytes 25165832 | tf_op jit(solution)/shard_map/ppermute | solution.py:21
  345.6 8.3 copy-start
  345.6 11.0 copy-start.1
  345.6 11.3 copy-start.3
  356.6 787.4 %collective-permute-start.3 = (bf16[8,128,8192]{2,1,0:T(8,128)(2,1)}, bf16[8,128,8192]{2,1,0:T(8,128)(2,1)}, u32[]{:S(2)}, u32[]{:S(2)}) collective-permute-start(bf16[8,128,8192]{2,1,0:T(8,128)(2,1)} %pad_maximum_fusion.1), channel_id=1, source_target_pairs={{0,16},{2,18},{4,20},{6,22},{8,24},{10,26},{12,28},{14,30},{16,0},... | collective-permute-start | bytes 50331656 | tf_op jit(solution)/shard_map/ppermute | solution.py:21
  360.5 7.5 copy-start.4
  360.5 858.5 %all-to-all-start.1 = ((bf16[192,16,1024]{2,0,1:T(8,128)(2,1)}), bf16[192,16,1024]{2,0,1:T(8,128)(2,1)}, u32[]{:S(2)}, u32[]{:S(2)}) async-start(bf16[192,16,1024]{2,0,1:T(8,128)(2,1)} %bitcast.42), calls=%async_computation.1 | async-start | bytes 12582912 | tf_op jit(solution)/shard_map/all_to_all | solution.py:67
  1222.5 150.1 %all-to-all-start = ((bf16[192,16,1024]{2,0,1:T(8,128)(2,1)}), bf16[192,16,1024]{2,0,1:T(8,128)(2,1)}, u32[]{:S(2)}, u32[]{:S(2)}) async-start(bf16[192,16,1024]{2,0,1:T(8,128)(2,1)} %bitcast.43), calls=%async_computation | async-start | bytes 12582912 | tf_op jit(solution)/shard_map/all_to_all | solution.py:68
